TPU v7x, 32 devices: a whole 2x2x4 slice. The times are simulated.
32 devices in a mesh: dp: 4 (over y, x), fsdp: 8 (over z, core).
Axes of the slice: x: 2, y: 2, z: 4, core: 2. Of those that a mesh axis runs over, the one named last changes fastest.
Arguments:
- activations: bfloat16 [4096, 4096], P('fsdp'), may hold values from -6 to 6
- cotangent: bfloat16 [4096, 14336], P('fsdp', 'dp'), may hold values from -6 to 6
- next_input: bfloat16 [4096, 4096], P('fsdp'), may hold values from -6 to 6
- next_weight: bfloat16 [4096, 14336], P('fsdp', 'dp'), may hold values from -0.09375 to 0.09375
- master: float32 [4096, 14336], P('fsdp', 'dp'), may hold values from -0.0625 to 0.0625
- first_moment: float32 [4096, 14336], P('fsdp', 'dp'), may hold values from -0.12 to 0.12
- second_moment: float32 [4096, 14336], P('fsdp', 'dp'), may hold values from 1e-05 to 0.0003
- token_counts: int32 [8], P('fsdp'), may hold values from 128 to 512, as said below
- peer_groups: int32 [4], replicated, may hold values from 0 to 3, as said below
Outputs:
- next_output: bfloat16 [4096, 14336], P('fsdp', 'dp')
- new_master: float32 [4096, 14336], P('fsdp', 'dp')
- new_first: float32 [4096, 14336], P('fsdp', 'dp')
- new_second: float32 [4096, 14336], P('fsdp', 'dp')
- copy_master: float32 [4096, 14336], P('fsdp', 'dp')
- copy_first: float32 [4096, 14336], P('fsdp', 'dp')
- copy_second: float32 [4096, 14336], P('fsdp', 'dp')
Inputs may be any that keep to these rules, and one draw needn't show every extreme that they name: token_counts[k] is the number of live rows in block k of 512 rows; rows at or past it are padding. peer_groups[g] = (g + s) mod 4 for one s from 1 to 3, the same s for every g.
All inputs are finite; a program needn't handle non-finite values.
Results may differ from a plain program's by a relative error of at most 0.025.
Values may be sent and summed in bfloat16 or wider, within the bound.
A program may use at most 192 MiB of HBM per device.

v0:
```python
from functools import partial

import jax
import jax.numpy as jnp
from jax import lax
from jax.sharding import PartitionSpec as P

beta_first = 0.9
beta_second = 0.95
epsilon = 1e-05
learn_rate = 0.00015
decay_rate = 0.1


def from_behind(shard, axis, by):
    size = lax.axis_size(axis)
    return lax.ppermute(shard, axis, [(i, (i + by) % size) for i in range(size)])


def adam_update(master, first_moment, second_moment, gradient):
    new_first = beta_first * first_moment + (1.0 - beta_first) * gradient
    new_second = beta_second * second_moment + (1.0 - beta_second) * gradient * gradient
    new_master = master - learn_rate * (
        new_first / (jnp.sqrt(new_second) + epsilon) + decay_rate * master
    )
    return (new_master, new_first, new_second)


def to_peer(sender, offset, groups):
    branches = [partial(sender, distance) for distance in range(1, groups)]
    return lax.switch(jnp.clip(offset - 1, 0, groups - 2), branches)


def body(
    activations,
    cotangent,
    next_input,
    next_weight,
    master,
    first_moment,
    second_moment,
    token_counts,
    peer_groups,
):
    groups = lax.axis_size("dp")
    offset = peer_groups[0]
    own_count = token_counts[0]
    token_total = lax.psum(own_count, "fsdp")
    positions = lax.broadcasted_iota(jnp.int32, (cotangent.shape[0], 1), 0)
    masked = jnp.where(positions < own_count, cotangent, jnp.zeros((), cotangent.dtype))
    feature_block = activations
    grad_sum = lax.psum_scatter(
        lax.dot_general(
            feature_block, masked, (((0,), (0,)), ((), ())), preferred_element_type=jnp.float32
        ).astype(jnp.bfloat16),
        "fsdp",
        scatter_dimension=0,
        tiled=True,
    ).astype(jnp.float32)
    feature_block = next_input
    forward = jnp.dot(
        feature_block,
        lax.all_gather(next_weight, "fsdp", axis=0, tiled=True),
        preferred_element_type=jnp.float32,
    )
    gradient = grad_sum / token_total.astype(jnp.float32)
    new_master, new_first, new_second = adam_update(master, first_moment, second_moment, gradient)
    copies = to_peer(
        lambda distance: (
            from_behind(new_master.astype(jnp.bfloat16), "dp", distance).astype(new_master.dtype),
            from_behind(new_first.astype(jnp.bfloat16), "dp", distance).astype(new_first.dtype),
            from_behind(new_second.astype(jnp.bfloat16), "dp", distance).astype(new_second.dtype),
        ),
        offset,
        groups,
    )
    return (
        forward.astype(jnp.bfloat16),
        new_master,
        new_first,
        new_second,
        copies[0],
        copies[1],
        copies[2],
    )


def solution(mesh):
    return jax.shard_map(
        body,
        mesh=mesh,
        in_specs=(
            P("fsdp", None),
            P("fsdp", "dp"),
            P("fsdp", None),
            P("fsdp", "dp"),
            P("fsdp", "dp"),
            P("fsdp", "dp"),
            P("fsdp", "dp"),
            P("fsdp"),
            P(),
        ),
        out_specs=(
            P("fsdp", "dp"),
            P("fsdp", "dp"),
            P("fsdp", "dp"),
            P("fsdp", "dp"),
            P("fsdp", "dp"),
            P("fsdp", "dp"),
            P("fsdp", "dp"),
        ),
        check_vma=False,
    )
```

profile of v0, /device:TPU:8, one launch (start us, length us, event | category | flops | bytes accessed | tf_op | source)
XLA Modules:
  0.0 855.0 jit_solution(12072878251650094577)
XLA Ops:
  8.6 22.1 %fusion = bf16[4096,3584]{0,1:T(8,128)(2,1)} fusion(bf16[512,4096]{1,0:T(8,128)(2,1)} %param.12, bf16[512,3584]{1,0:T(8,128)(2,1)} %param.13, pred[512]{0:T(512)(128)(4,1)S(1)} %iota_compare_fusion), kind=kOutput, calls=%fused_computation.1 | convolution fusion | flops 15048900608 | bytes 37224960 | tf_op jit(solution)/shard_map/dot_general | solution.py:53
  30.7 17.5 %psum.7 = s32[]{:T(128)} all-reduce(s32[]{:T(128)} %bitcast), channel_id=1, replica_groups=mesh['dp'=4,'fsdp'=8] {'fsdp'}, use_global_device_ids=true, to_apply=%region_1.2 | all-reduce | flops 1 | bytes 8 | tf_op jit(solution)/shard_map/psum | solution.py:48
  48.2 8.4 copy.16
  56.6 8.4 copy.17
  65.0 8.4 copy.19
  74.1 188.2 %all-gather.2.cloned.1.call-done = bf16[4096,3584]{1,0:T(8,128)(2,1)} async-done(((bf16[512,3584]{1,0:T(8,128)(2,1)}), bf16[4096,3584]{1,0:T(8,128)(2,1)}) %all-gather.2.cloned.1.call-update) | async-done | bytes 29360144 | tf_op jit(solution)/shard_map/all_gather | solution.py:63
  262.3 23.2 %convolution_convert_fusion.1 = bf16[512,3584]{1,0:T(8,128)(2,1)} fusion(bf16[512,4096]{1,0:T(8,128)(2,1)} %param.14, bf16[4096,3584]{1,0:T(8,128)(2,1)} %all-gather.2.cloned.1.call-done), kind=kOutput, calls=%fused_computation.7 | convolution fusion | flops 15034220544 | bytes 37224448 | tf_op jit(solution)/shard_map/dot_general | solution.py:61
  285.4 264.2 %reduce-scatter.2.cloned.1.call-done = bf16[512,3584]{0,1:T(8,128)(2,1)} async-done(((bf16[4096,3584]{0,1:T(8,128)(2,1)}), bf16[512,3584]{0,1:T(8,128)(2,1)}) %reduce-scatter.2.cloned.1.call-update) | async-done | bytes 3670032 | tf_op jit(solution)/shard_map/reduce_scatter | solution.py:52
  549.6 18.3 %multiply_subtract_fusion = (f32[512,3584]{0,1:T(8,128)}, f32[512,3584]{0,1:T(8,128)}, f32[512,3584]{0,1:T(8,128)}) fusion(f32[512,3584]{0,1:T(8,128)} %copy.19, f32[]{:T(128)S(6)} %convert_element_type.97, bf16[512,3584]{0,1:T(8,128)(2,1)} %reduce-scatter.2.cloned.1.call-done, f32[512,3584]{0,1:T(8,128)} %copy.17, f32[512,3584]{0,1:T(8,128)} %copy.16), kind=kLoop, calls=%fused_computation.4 | loop fusion | flops 27525120 | bytes 47710212 | tf_op jit(solution)/shard_map/sub | solution.py:23
  567.9 8.4 copy.29
  576.2 8.4 copy.30
  584.6 8.4 copy.31
  593.0 247.6 %conditional.4 = (f32[512,3584]{1,0:T(8,128)S(1)}, f32[512,3584]{1,0:T(8,128)S(1)}, f32[512,3584]{1,0:T(8,128)S(1)}) conditional(s32[]{:T(128)} %bitcast.2, (f32[512,3584]{0,1:T(8,128)}, f32[512,3584]{0,1:T(8,128)}, f32[512,3584]{0,1:T(8,128)}) %tuple.46, (f32[512,3584]{0,1:T(8,128)}, f32[512,3584]{0,1:T(8,128)}, ...), branch_computations={%region_2.3_spmd, %region_3.4_spmd, %region_4.5_spmd} | conditional | flops 5505024 | bytes 110100624
  593.0 6.9 copy.26
  599.9 2.5 collective-permute-start.6
  602.3 6.9 copy.27
  609.8 6.9 copy.28
  618.2 64.1 %collective-permute-done.6 = bf16[512,3584]{1,0:T(8,128)(2,1)} collective-permute-done((bf16[512,3584]{1,0:T(8,128)(2,1)}, bf16[512,3584]{1,0:T(8,128)(2,1)}, u32[]{:S(2)}, u32[]{:S(2)}) %collective-permute-start.6) | collective-permute-done | bytes 3670048 | tf_op jit(solution)/shard_map/cond/branch_2_fun/ppermute | solution.py:17
  682.3 3.0 convert_element_type.103
  685.2 75.7 %collective-permute-done.7 = bf16[512,3584]{1,0:T(8,128)(2,1)} collective-permute-done((bf16[512,3584]{1,0:T(8,128)(2,1)}, bf16[512,3584]{1,0:T(8,128)(2,1)}, u32[]{:S(2)}, u32[]{:S(2)}) %collective-permute-start.7) | collective-permute-done | bytes 3670048 | tf_op jit(solution)/shard_map/cond/branch_2_fun/ppermute | solution.py:17
  760.9 3.0 convert_element_type.106
  763.9 75.7 %collective-permute-done.8 = bf16[512,3584]{1,0:T(8,128)(2,1)S(1)} collective-permute-done((bf16[512,3584]{1,0:T(8,128)(2,1)}, bf16[512,3584]{1,0:T(8,128)(2,1)S(1)}, u32[]{:S(2)}, u32[]{:S(2)}) %collective-permute-start.8) | collective-permute-done | bytes 3670048 | tf_op jit(solution)/shard_map/cond/branch_2_fun/ppermute | solution.py:17
  840.5 3.0 copy-done
  843.6 2.4 copy-done.1
  (14 shorter events, 6.0 us)
Async XLA Ops:
  7.2 255.1 %all-gather.2.cloned.1.call-start = ((), (), s32[]{:S(2)}) async-start(), calls=%async_computation.1 | async-start | bytes 33030144 | tf_op jit(solution)/shard_map/all_gather | solution.py:63
  7.9 541.7 %reduce-scatter.2.cloned.1.call-start = ((), (), s32[]{:S(2)}) async-start(), calls=%async_computation.2 | async-start | bytes 33030144 | tf_op jit(solution)/shard_map/reduce_scatter | solution.py:52
  65.0 9.1 %copy-start.3 = (s32[4]{0:T(128)S(1)}, s32[4]{0:T(128)}, u32[]{:S(2)}) copy-start(s32[4]{0:T(128)} %param.20) | copy-start | bytes 52
  599.9 82.4 %collective-permute-start.6 = (bf16[512,3584]{1,0:T(8,128)(2,1)}, bf16[512,3584]{1,0:T(8,128)(2,1)}, u32[]{:S(2)}, u32[]{:S(2)}) collective-permute-start(bf16[512,3584]{1,0:T(8,128)(2,1)} %copy.26), channel_id=1, source_target_pairs={{0,24},{8,0},{16,8},{24,16},{1,25},{9,1},{17,9},{25,17},{2,26},{10... | collective-permute-start | bytes 11010056 | tf_op jit(solution)/shard_map/cond/branch_2_fun/ppermute | solution.py:17
  609.3 151.7 %collective-permute-start.7 = (bf16[512,3584]{1,0:T(8,128)(2,1)}, bf16[512,3584]{1,0:T(8,128)(2,1)}, u32[]{:S(2)}, u32[]{:S(2)}) collective-permute-start(bf16[512,3584]{1,0:T(8,128)(2,1)} %copy.27), channel_id=1, source_target_pairs={{0,24},{8,0},{16,8},{24,16},{1,25},{9,1},{17,9},{25,17},{2,26},{10... | collective-permute-start | bytes 11010056 | tf_op jit(solution)/shard_map/cond/branch_2_fun/ppermute | solution.py:17
  616.7 222.8 %collective-permute-start.8 = (bf16[512,3584]{1,0:T(8,128)(2,1)}, bf16[512,3584]{1,0:T(8,128)(2,1)S(1)}, u32[]{:S(2)}, u32[]{:S(2)}) collective-permute-start(bf16[512,3584]{1,0:T(8,128)(2,1)} %copy.28), channel_id=1, source_target_pairs={{0,24},{8,0},{16,8},{24,16},{1,25},{9,1},{17,9},{25,17},{2,26},{10... | collective-permute-start | bytes 11010056 | tf_op jit(solution)/shard_map/cond/branch_2_fun/ppermute | solution.py:17
  840.5 3.1 copy-start
  840.5 5.5 copy-start.1
  840.5 7.7 copy-start.2
Sparse Core Ops, SparseCore 0:
  9.6 252.5 all-gather.1
  264.6 284.9 reduce-scatter.1
where the time goes:
time: 857 us; the launch traced here: 855 us
  waiting for transfers between devices  668 us (78%)
  local copies, waits for them, and re-layouts  78.7 us (9%)
  matrix products  45.2 us (5%)
  other arithmetic  25.2 us (3%)
  blocking collectives  17.5 us (2%)
  between operations  15.4 us (2%)
    reduce_scatter x1, waiting for transfers between devices, body(): lax.psum_scatter(lax.dot_general(feature_block, masked, (((0,), (0,)), ((...  264 us
    ppermute x3, waiting for transfers between devices, from_behind(): lax.ppermute(shard, axis, [(i, (i + by) % size) for i in range(size)])  215 us
    all_gather x1, waiting for transfers between devices, body(): lax.all_gather(next_weight, 'fsdp', axis=0, tiled=True)  188 us
    unnamed x14, local copies, waits for them, and re-layouts  57.9 us
    dot_general x1, matrix products, body(): jnp.dot(feature_block, lax.all_gather(next_weight, 'fsdp', axis=0, tiled=...  23.2 us
    dot_general x1, matrix products, body(): lax.dot_general(feature_block, masked, (((0,), (0,)), ((), ())), preferre...  22.1 us
    another operation x3, local copies, waits for them, and re-layouts  20.8 us
    sub x1, other arithmetic, adam_update(): master - learn_rate * (new_first / (jnp.sqrt(new_second) + epsilon) + dec...  18.3 us
  transfers between devices with their start and end apart: 5, of which 5 were waited for; matrix products, arithmetic and copies ran while one was open for 11% of the time, Pallas kernels for 0%

commit v1 on v0

--- a/solution.py
+++ b/solution.py
@@ -3,6 +3,7 @@
 import jax
 import jax.numpy as jnp
 from jax import lax
+from jax.experimental.layout import Layout, with_layout_constraint
 from jax.sharding import PartitionSpec as P
 
 beta_first = 0.9
@@ -48,21 +49,14 @@
     token_total = lax.psum(own_count, "fsdp")
     positions = lax.broadcasted_iota(jnp.int32, (cotangent.shape[0], 1), 0)
     masked = jnp.where(positions < own_count, cotangent, jnp.zeros((), cotangent.dtype))
-    feature_block = activations
-    grad_sum = lax.psum_scatter(
-        lax.dot_general(
-            feature_block, masked, (((0,), (0,)), ((), ())), preferred_element_type=jnp.float32
-        ).astype(jnp.bfloat16),
-        "fsdp",
-        scatter_dimension=0,
-        tiled=True,
-    ).astype(jnp.float32)
-    feature_block = next_input
-    forward = jnp.dot(
-        feature_block,
-        lax.all_gather(next_weight, "fsdp", axis=0, tiled=True),
-        preferred_element_type=jnp.float32,
-    )
+    partial_sums = lax.dot_general(
+        activations, masked, (((0,), (0,)), ((), ())), preferred_element_type=jnp.float32
+    ).astype(jnp.bfloat16)
+    partial_sums = with_layout_constraint(partial_sums, Layout((0, 1)))
+    grad_sum = lax.psum_scatter(partial_sums, "fsdp", scatter_dimension=0, tiled=True)
+    grad_sum, next_weight = lax.optimization_barrier((grad_sum, next_weight))
+    grad_sum = grad_sum.astype(jnp.float32)
+    gathered = lax.all_gather(next_weight, "fsdp", axis=0, tiled=True)
     gradient = grad_sum / token_total.astype(jnp.float32)
     new_master, new_first, new_second = adam_update(master, first_moment, second_moment, gradient)
     copies = to_peer(
@@ -74,8 +68,10 @@
         offset,
         groups,
     )
+    gathered, copies = lax.optimization_barrier((gathered, copies))
+    forward = jnp.dot(next_input, gathered, preferred_element_type=jnp.float32)
     return (
-        forward.astype(jnp.bfloat16),
+        with_layout_constraint(forward.astype(jnp.bfloat16), Layout((0, 1))),
         new_master,
         new_first,
         new_second,

time: 857 us -> 624 us (0.73)
  waiting for transfers between devices: 668 us -> 503 us
  local copies, waits for them, and re-layouts: 78.7 us -> 0.01 us
  other arithmetic: 25.2 us -> 44 us
    all_gather x1, waiting for transfers between devices: 188 us -> 0.01 us  [body(): gathered = lax.all_gather(next_weight, 'fsdp', axis=0, tiled=True)]
    unnamed x14 -> x2, local copies, waits for them, and re-layouts: 57.9 us -> 0.01 us
    reduce_scatter x1, waiting for transfers between devices: 264 us -> 285 us  [body(): lax.psum_scatter(partial_sums, 'fsdp', scatter_dimension=0, tiled=True)]
    another operation x3 -> x0, local copies, waits for them, and re-layouts: 20.8 us -> none
    convert_element_type x0 -> x3, other arithmetic: none -> 10.6 us  [the longest x1 3.56 us: body(): new_first.astype(jnp.bfloat16)]
  transfers between devices with their start and end apart: 5 -> 5, of which waited for: 5 -> 4; matrix products, arithmetic and copies ran while one was open for 11% -> 7% of each run, Pallas kernels for 0% -> 0%
where the time goes in v1:
time: 624 us; the launch traced here: 622 us
  waiting for transfers between devices  503 us (81%)
  matrix products  45.7 us (7%)
  other arithmetic  44 us (7%)
  between operations  15.4 us (2%)
  blocking collectives  9.24 us (1%)
    reduce_scatter x1, waiting for transfers between devices, body(): lax.psum_scatter(partial_sums, 'fsdp', scatter_dimension=0, tiled=True)  285 us
    ppermute x3, waiting for transfers between devices, from_behind(): lax.ppermute(shard, axis, [(i, (i + by) % size) for i in range(size)])  218 us
    dot_general x1, matrix products, body(): forward = jnp.dot(next_input, gathered, preferred_element_type=jnp.float32)  23.2 us
    dot_general x1, matrix products, body(): lax.dot_general(activations, masked, (((0,), (0,)), ((), ())), preferred_...  22.5 us
    sub x1, other arithmetic, adam_update(): master - learn_rate * (new_first / (jnp.sqrt(new_second) + epsilon) + dec...  21.4 us
  transfers between devices with their start and end apart: 5, of which 4 were waited for; matrix products, arithmetic and copies ran while one was open for 7% of the time, Pallas kernels for 0%

profile of v1, /device:TPU:8, one launch (start us, length us, event | category | flops | bytes accessed | tf_op | source)
XLA Modules:
  0.0 622.5 jit_solution(9339656046601393395)
XLA Ops:
  7.2 0.0 reduce-scatter.2.cloned.1.call-start
  7.9 22.5 %fusion = bf16[4096,3584]{1,0:T(8,128)(2,1)} fusion(bf16[512,4096]{1,0:T(8,128)(2,1)} %param.12, bf16[512,3584]{1,0:T(8,128)(2,1)} %param.13, pred[512]{0:T(512)(128)(4,1)S(1)} %iota_compare_fusion), kind=kOutput, calls=%fused_computation.1 | convolution fusion | flops 15048900608 | bytes 37224960 | tf_op jit(solution)/shard_map/dot_general | solution.py:52
  30.4 0.0 copy-start
  30.4 0.0 reduce-scatter.2.cloned.1.call-update
  30.4 0.0 all-gather.2.cloned.1.call-start
  30.4 285.0 %reduce-scatter.2.cloned.1.call-done = bf16[512,3584]{1,0:T(8,128)(2,1)} async-done(((bf16[4096,3584]{1,0:T(8,128)(2,1)}), bf16[512,3584]{1,0:T(8,128)(2,1)}) %reduce-scatter.2.cloned.1.call-update) | async-done | bytes 3670032 | tf_op jit(solution)/shard_map/reduce_scatter | solution.py:56
  315.5 0.0 all-gather.2.cloned.1.call-update
  315.5 9.2 %psum.7 = s32[]{:T(128)} all-reduce(s32[]{:T(128)} %bitcast), channel_id=1, replica_groups=mesh['dp'=4,'fsdp'=8] {'fsdp'}, use_global_device_ids=true, to_apply=%region_1.2 | all-reduce | flops 1 | bytes 8 | tf_op jit(solution)/shard_map/psum | solution.py:49
  325.4 0.0 copy-done
  325.5 21.4 %multiply_subtract_fusion = (f32[512,3584]{1,0:T(8,128)}, f32[512,3584]{1,0:T(8,128)}, f32[512,3584]{1,0:T(8,128)}) fusion(f32[512,3584]{1,0:T(8,128)} %param.16, f32[]{:T(128)S(6)} %convert_element_type.99, bf16[512,3584]{1,0:T(8,128)(2,1)} %reduce-scatter.2.cloned.1.call-done, f32[512,3584]{1,0:T(8,128)} %param.18, f32[512,3584]{1,0:T(8,128)} %param.17), kind=kLoop, calls=%fused_computation.4 | loop fusion | flops 27525120 | bytes 47710212 | tf_op jit(solution)/shard_map/sub | solution.py:24
  346.9 245.6 %conditional.4 = (f32[512,3584]{1,0:T(8,128)}, f32[512,3584]{1,0:T(8,128)}, f32[512,3584]{1,0:T(8,128)}) conditional(s32[]{:T(128)} %bitcast.2, (f32[512,3584]{1,0:T(8,128)}, f32[512,3584]{1,0:T(8,128)}, f32[512,3584]{1,0:T(8,128)}) %tuple.49, (f32[512,3584]{1,0:T(8,128)}, f32[512,3584]{1,0:T(8,128)}, ...), branch_computations={%region_2.3_spmd, %region_3.4_spmd, %region_4.5_spmd} | conditional | flops 11010048 | bytes 110100624
  346.9 3.5 convert_element_type.72
  350.4 1.5 collective-permute-start
  351.9 3.6 convert_element_type.74
  355.5 1.6 collective-permute-start.1
  357.1 3.5 convert_element_type.76
  360.6 1.5 collective-permute-start.2
  362.1 71.5 %collective-permute-done = bf16[512,3584]{1,0:T(8,128)(2,1)S(1)} collective-permute-done((bf16[512,3584]{1,0:T(8,128)(2,1)S(1)}, bf16[512,3584]{1,0:T(8,128)(2,1)S(1)}, u32[]{:S(2)}, u32[]{:S(2)}) %collective-permute-start) | collective-permute-done | bytes 3670048 | tf_op jit(solution)/shard_map/cond/branch_0_fun/ppermute | solution.py:18
  433.6 4.0 convert_element_type.105
  437.6 74.6 %collective-permute-done.1 = bf16[512,3584]{1,0:T(8,128)(2,1)S(1)} collective-permute-done((bf16[512,3584]{1,0:T(8,128)(2,1)S(1)}, bf16[512,3584]{1,0:T(8,128)(2,1)S(1)}, u32[]{:S(2)}, u32[]{:S(2)}) %collective-permute-start.1) | collective-permute-done | bytes 3670048 | tf_op jit(solution)/shard_map/cond/branch_0_fun/ppermute | solution.py:18
  512.3 4.0 convert_element_type.108
  516.3 72.2 %collective-permute-done.2 = bf16[512,3584]{1,0:T(8,128)(2,1)S(1)} collective-permute-done((bf16[512,3584]{1,0:T(8,128)(2,1)S(1)}, bf16[512,3584]{1,0:T(8,128)(2,1)S(1)}, u32[]{:S(2)}, u32[]{:S(2)}) %collective-permute-start.2) | collective-permute-done | bytes 3670048 | tf_op jit(solution)/shard_map/cond/branch_0_fun/ppermute | solution.py:18
  588.5 4.0 convert_element_type.111
  592.5 23.2 %fusion.2 = bf16[512,3584]{1,0:T(8,128)(2,1)} fusion(bf16[512,4096]{1,0:T(8,128)(2,1)} %param.14, bf16[4096,3584]{1,0:T(8,128)(2,1)} %all-gather.2.cloned.1.call-done), kind=kOutput, calls=%fused_computation.8 | convolution fusion | flops 15034220544 | bytes 37224448 | tf_op jit(solution)/shard_map/dot_general | solution.py:72
  (2 shorter events, 0.0 us)
Async XLA Ops:
  7.2 308.3 %reduce-scatter.2.cloned.1.call-start = ((), (), s32[]{:S(2)}) async-start(), calls=%async_computation.1 | async-start | bytes 33030144 | tf_op jit(solution)/shard_map/reduce_scatter | solution.py:56
  30.4 295.0 %copy-start = (s32[4]{0:T(128)S(1)}, s32[4]{0:T(128)}, u32[]{:S(2)}) copy-start(s32[4]{0:T(128)} %param.20) | copy-start | bytes 52
  30.4 562.1 %all-gather.2.cloned.1.call-start = ((), (), s32[]{:S(2)}) async-start(), calls=%async_computation.2 | async-start | bytes 33030144 | tf_op jit(solution)/shard_map/all_gather | solution.py:59
  350.4 83.2 %collective-permute-start = (bf16[512,3584]{1,0:T(8,128)(2,1)S(1)}, bf16[512,3584]{1,0:T(8,128)(2,1)S(1)}, u32[]{:S(2)}, u32[]{:S(2)}) collective-permute-start(bf16[512,3584]{1,0:T(8,128)(2,1)S(1)} %convert_element_type.72), channel_id=1, source_target_pairs={{0,8},{8,16},{16,24},{24,0},{1,9},{9,17},{17,25},{25,1},{2,10},{10... | collective-permute-start | bytes 11010056 | tf_op jit(solution)/shard_map/cond/branch_0_fun/ppermute | solution.py:18
  355.5 156.8 %collective-permute-start.1 = (bf16[512,3584]{1,0:T(8,128)(2,1)S(1)}, bf16[512,3584]{1,0:T(8,128)(2,1)S(1)}, u32[]{:S(2)}, u32[]{:S(2)}) collective-permute-start(bf16[512,3584]{1,0:T(8,128)(2,1)S(1)} %convert_element_type.74), channel_id=1, source_target_pairs={{0,8},{8,16},{16,24},{24,0},{1,9},{9,17},{17,25},{25,1},{2,10},{10... | collective-permute-start | bytes 11010056 | tf_op jit(solution)/shard_map/cond/branch_0_fun/ppermute | solution.py:18
  360.6 227.9 %collective-permute-start.2 = (bf16[512,3584]{1,0:T(8,128)(2,1)S(1)}, bf16[512,3584]{1,0:T(8,128)(2,1)S(1)}, u32[]{:S(2)}, u32[]{:S(2)}) collective-permute-start(bf16[512,3584]{1,0:T(8,128)(2,1)S(1)} %convert_element_type.76), channel_id=1, source_target_pairs={{0,8},{8,16},{16,24},{24,0},{1,9},{9,17},{17,25},{25,1},{2,10},{10... | collective-permute-start | bytes 11010056 | tf_op jit(solution)/shard_map/cond/branch_0_fun/ppermute | solution.py:18
Sparse Core Ops, SparseCore 0:
  30.5 284.9 reduce-scatter.1
  317.1 252.4 all-gather.1

commit v2 on v1

v2 whole, which is shorter than its diff:
```python
from functools import partial

import jax
import jax.numpy as jnp
from jax import lax
from jax.experimental import pallas as pl
from jax.experimental.layout import Layout, with_layout_constraint
from jax.experimental.pallas import tpu as pltpu
from jax.sharding import PartitionSpec as P

beta_first = 0.9
beta_second = 0.95
epsilon = 1e-05
learn_rate = 0.00015
decay_rate = 0.1

MESH = pl.DeviceIdType.MESH
WIDTH = 256
HOP = 2
PARTS = 8


def adam_update(master, first_moment, second_moment, gradient):
    new_first = beta_first * first_moment + (1.0 - beta_first) * gradient
    new_second = beta_second * second_moment + (1.0 - beta_second) * gradient * gradient
    new_master = master - learn_rate * (
        new_first / (jnp.sqrt(new_second) + epsilon) + decay_rate * master
    )
    return (new_master, new_first, new_second)


def kernel(
    chips, groups, chunks, distance,
    total, sums, weight, master, first, second,
    gathered, out_master, out_first, out_second, copies,
    paired, arrived, own, state, fresh, staged,
    pair_send, pair_recv, line_send, line_recv, gather_send, gather_recv,
    twin_send, twin_recv, copy_send, copy_recv, own_sem, state_sem, fresh_sem, keep_sem,
):
    g = lax.axis_index("dp")
    f = lax.axis_index("fsdp")
    z = f // 2
    core = f % 2
    rows = weight.shape[0]
    piece = rows // PARTS
    last = chips - 1
    finish = 1 + HOP * last
    twin = (g, z * 2 + 1 - core)
    right = (g, ((z + 1) % chips) * 2 + core)
    left = (g, ((z + chips - 1) % chips) * 2 + core)
    peer = ((g + distance) % groups, f)
    giver = ((g + groups - distance) % groups, f)

    def cols(c):
        return pl.ds(pl.multiple_of(c * WIDTH, WIDTH), WIDTH)

    def remote(src, dst, send, recv, device):
        return pltpu.make_async_remote_copy(
            src_ref=src, dst_ref=dst, send_sem=send, recv_sem=recv,
            device_id=device, device_id_type=MESH,
        )

    def pair_copy(c):
        return remote(sums.at[:, 1 - core, :, cols(c)], paired.at[c],
                      pair_send.at[c], pair_recv.at[c], twin)

    def own_load(c):
        return pltpu.make_async_copy(sums.at[:, core, :, cols(c)], own.at[c % 3], own_sem.at[c % 3])

    def line_copy(c, d, slot, device):
        return remote(paired.at[c, d], arrived.at[c, slot],
                      line_send.at[c, d], line_recv.at[c, slot], device)

    def first_gather(c, way, device):
        return remote(weight.at[:, cols(c)], gathered.at[z, core, :, cols(c)],
                      gather_send.at[c, chips if way else z], gather_recv.at[c, z], device)

    def gather_copy(c, o, device):
        part = gathered.at[o, core, :, cols(c)]
        return remote(part, part, gather_send.at[c, o], gather_recv.at[c, o], device)

    def first_twin(c):
        return remote(weight.at[:, cols(c)], gathered.at[z, core, :, cols(c)],
                      twin_send.at[c, z], twin_recv.at[c, z], twin)

    def twin_copy(c, o):
        part = gathered.at[o, core, :, cols(c)]
        return remote(part, part, twin_send.at[c, o], twin_recv.at[c, o], twin)

    def twin_arrival(c, o):
        part = gathered.at[o, 1 - core, :, cols(c)]
        return remote(part, part, twin_send.at[c, o], twin_recv.at[c, o], twin)

    def peer_copy(c):
        return remote(staged.at[c], copies.at[:, :, cols(c)], copy_send.at[c], copy_recv.at[c], peer)

    def state_loads(c):
        return [
            pltpu.make_async_copy(ref.at[:, cols(c)], state.at[c % 2, i], state_sem.at[c % 2, i])
            for i, ref in enumerate((master, first, second))
        ]

    def fresh_stores(c):
        return [
            pltpu.make_async_copy(fresh.at[c % 2, i], ref.at[:, cols(c)], fresh_sem.at[c % 2, i])
            for i, ref in enumerate((out_master, out_first, out_second))
        ]

    def add_into(c, d, ref):
        @pl.loop(0, PARTS)
        def _(i):
            part = pl.ds(pl.multiple_of(i * piece, piece), piece)
            total_part = paired[c, d, part, :].astype(jnp.float32) + ref[part, :].astype(jnp.float32)
            paired[c, d, part, :] = total_part.astype(jnp.bfloat16)

    barrier = pltpu.get_barrier_semaphore()

    greeted = (twin, peer, giver, left, right)
    for device in greeted:
        pl.semaphore_signal(barrier, inc=1, device_id=device, device_id_type=MESH)
    pl.semaphore_wait(barrier, len(greeted))

    keep = pltpu.make_async_copy(weight, gathered.at[z, core], keep_sem)
    keep.start()
    pair_copy(0).start()
    own_load(0).start()

    def within(c):
        return jnp.logical_and(c >= 0, c < chunks)

    @pl.loop(0, chunks + finish)
    def _(t):
        @pl.when(t + 1 < chunks)
        def _():
            pair_copy(t + 1).start()
            own_load(t + 1).start()

        @pl.when(t < chunks)
        def _():
            @pl.when(z < last)
            def _():
                first_gather(t, 0, right).start()

            @pl.when(z > 0)
            def _():
                first_gather(t, 1, left).start()

            first_twin(t).start()

        for o in range(chips):
            from_left = t - HOP * (z - o)
            from_right = t - HOP * (o - z)

            @pl.when(jnp.logical_and(z > o, within(from_left)))
            def _():
                gather_copy(from_left, o, left).wait_recv()

                @pl.when(z < last)
                def _():
                    gather_copy(from_left, o, right).start()

                twin_copy(from_left, o).start()

            @pl.when(jnp.logical_and(z < o, within(from_right)))
            def _():
                gather_copy(from_right, o, right).wait_recv()

                @pl.when(z > 0)
                def _():
                    gather_copy(from_right, o, left).start()

                twin_copy(from_right, o).start()

        joined = t - 1

        @pl.when(within(joined))
        def _():
            pair_copy(joined).wait_recv()
            own_load(joined).wait()
            for d in range(chips):
                add_into(joined, d, own.at[joined % 3, d])

        rightward = t - 1 - HOP * z

        @pl.when(within(rightward))
        def _():
            for d in range(chips):
                @pl.when(z <= d)
                def _():
                    @pl.when(z > 0)
                    def _():
                        line_copy(rightward, d, d, left).wait_recv()
                        add_into(rightward, d, arrived.at[rightward, d])

                    @pl.when(z < d)
                    def _():
                        line_copy(rightward, d, d, right).start()

        leftward = t - 1 - HOP * (last - z)

        @pl.when(within(leftward))
        def _():
            for d in range(chips):
                @pl.when(z >= d)
                def _():
                    @pl.when(z < last)
                    def _():
                        @pl.when(z > d)
                        def _():
                            line_copy(leftward, d, d, right).wait_recv()
                            add_into(leftward, d, arrived.at[leftward, d])

                        @pl.when(z == d)
                        def _():
                            line_copy(leftward, d, chips, right).wait_recv()
                            add_into(leftward, d, arrived.at[leftward, chips])

                    @pl.when(z == d + 1)
                    def _():
                        line_copy(leftward, d, chips, left).start()

                    @pl.when(z > d + 1)
                    def _():
                        line_copy(leftward, d, d, left).start()

        coming = t + 1 - finish

        @pl.when(within(coming))
        def _():
            for copy in state_loads(coming):
                copy.start()

        done = t - finish

        @pl.when(within(done))
        def _():
            for copy in state_loads(done):
                copy.wait()

            @pl.when(done >= 2)
            def _():
                for copy in fresh_stores(done - 2):
                    copy.wait()

            slot = done % 2

            @pl.loop(0, PARTS)
            def _(i):
                part = pl.ds(pl.multiple_of(i * piece, piece), piece)
                gradient = paired[done, z, part, :].astype(jnp.float32) / total[0]
                results = adam_update(
                    state[slot, 0, part, :], state[slot, 1, part, :], state[slot, 2, part, :], gradient
                )
                for k, value in enumerate(results):
                    fresh[slot, k, part, :] = value
                    staged[done, k, part, :] = value.astype(jnp.bfloat16)

            peer_copy(done).start()
            for copy in fresh_stores(done):
                copy.start()

    keep.wait()
    for c in range(max(chunks - 2, 0), chunks):
        for copy in fresh_stores(c):
            copy.wait()

    @pl.loop(0, chunks)
    def _(c):
        pair_copy(c).wait_send()
        peer_copy(c).wait()
        first_twin(c).wait_send()

        @pl.when(z < last)
        def _():
            first_gather(c, 0, right).wait_send()

        @pl.when(z > 0)
        def _():
            first_gather(c, 1, left).wait_send()

        for o in range(chips):
            twin_arrival(c, o).wait_recv()

            @pl.when(z != o)
            def _():
                twin_copy(c, o).wait_send()
                line_copy(c, o, o, right).wait_send()

            @pl.when(jnp.logical_and(z > o, z < last))
            def _():
                gather_copy(c, o, right).wait_send()

            @pl.when(jnp.logical_and(z < o, z > 0))
            def _():
                gather_copy(c, o, left).wait_send()


def exchange(distance, total, sums, weight, master, first, second):
    groups, members = lax.axis_size("dp"), lax.axis_size("fsdp")
    rows, columns = weight.shape
    chips, chunks = members // 2, columns // WIDTH
    whole = pl.BlockSpec(memory_space=pl.ANY)
    dma = pltpu.SemaphoreType.DMA
    block = (rows, WIDTH)
    gathered, new_master, new_first, new_second, copies = pl.pallas_call(
        partial(kernel, chips, groups, chunks, distance),
        out_shape=(
            jax.ShapeDtypeStruct((chips, 2, rows, columns), weight.dtype),
            jax.ShapeDtypeStruct(master.shape, master.dtype),
            jax.ShapeDtypeStruct(first.shape, first.dtype),
            jax.ShapeDtypeStruct(second.shape, second.dtype),
            jax.ShapeDtypeStruct((3, rows, columns), jnp.bfloat16),
        ),
        in_specs=[pl.BlockSpec(memory_space=pltpu.SMEM)] + [whole] * 5,
        out_specs=(whole,) * 5,
        scratch_shapes=[
            pltpu.VMEM((chunks, chips) + block, jnp.bfloat16),
            pltpu.VMEM((chunks, chips + 1) + block, jnp.bfloat16),
            pltpu.VMEM((3, chips) + block, jnp.bfloat16),
            pltpu.VMEM((2, 3) + block, jnp.float32),
            pltpu.VMEM((2, 3) + block, jnp.float32),
            pltpu.VMEM((chunks, 3) + block, jnp.bfloat16),
            dma((chunks,)), dma((chunks,)),
            dma((chunks, chips)), dma((chunks, chips + 1)),
            dma((chunks, chips + 1)), dma((chunks, chips)),
            dma((chunks, chips)), dma((chunks, chips)),
            dma((chunks,)), dma((chunks,)),
            dma((3,)), dma((2, 3)), dma((2, 3)), dma(()),
        ],
        compiler_params=pltpu.CompilerParams(
            collective_id=distance, has_side_effects=True, vmem_limit_bytes=60 * 1024 * 1024
        ),
        name=f"exchange_{distance}",
    )(total, sums, weight, master, first, second)
    return (
        gathered, new_master, new_first, new_second,
        *(copies[i].astype(jnp.float32) for i in range(3)),
    )


def body(
    activations,
    cotangent,
    next_input,
    next_weight,
    master,
    first_moment,
    second_moment,
    token_counts,
    peer_groups,
):
    groups, members = lax.axis_size("dp"), lax.axis_size("fsdp")
    rows, columns = next_weight.shape
    own_count = token_counts[0]
    token_total = lax.psum(own_count, "fsdp").astype(jnp.float32).reshape(1)
    positions = lax.broadcasted_iota(jnp.int32, (cotangent.shape[0], 1), 0)
    masked = jnp.where(positions < own_count, cotangent, jnp.zeros((), cotangent.dtype))
    sums = lax.dot_general(
        activations, masked, (((0,), (0,)), ((), ())), preferred_element_type=jnp.float32
    ).astype(jnp.bfloat16)
    sums = with_layout_constraint(sums, Layout((0, 1))).reshape(members // 2, 2, rows, columns)
    branches = [partial(exchange, distance) for distance in range(1, groups)]
    gathered, *states = lax.switch(
        jnp.clip(peer_groups[0] - 1, 0, groups - 2), branches,
        token_total, sums, next_weight, master, first_moment, second_moment,
    )
    forward = jnp.dot(
        next_input, gathered.reshape(members * rows, columns), preferred_element_type=jnp.float32
    ).astype(jnp.bfloat16)
    return (with_layout_constraint(forward, Layout((0, 1))), *states)


def solution(mesh):
    return jax.shard_map(
        body,
        mesh=mesh,
        in_specs=(
            P("fsdp", None),
            P("fsdp", "dp"),
            P("fsdp", None),
            P("fsdp", "dp"),
            P("fsdp", "dp"),
            P("fsdp", "dp"),
            P("fsdp", "dp"),
            P("fsdp"),
            P(),
        ),
        out_specs=(P("fsdp", "dp"),) * 7,
        check_vma=False,
    )
```

time: 624 us -> 489 us (0.78)
  waiting for transfers between devices: 503 us -> 0 us
  Pallas kernels: 0 us -> 407 us
  other arithmetic: 44 us -> 9.29 us
  local copies, waits for them, and re-layouts: 0.01 us -> 13.8 us
  between operations: 15.4 us -> 2.62 us
    pallas_call x0 -> x1, Pallas kernels: none -> 407 us  [exchange(): pl.pallas_call(partial(kernel, chips, groups, chunks, distance), out_shap...]
    reduce_scatter x1 -> x0, waiting for transfers between devices: 285 us -> none  [body(): lax.psum_scatter(partial_sums, 'fsdp', scatter_dimension=0, tiled=True)]
    ppermute x3 -> x0, waiting for transfers between devices: 218 us -> none  [from_behind(): lax.ppermute(shard, axis, [(i, (i + by) % size) for i in range(size)])]
    sub x1 -> x0, other arithmetic: 21.4 us -> none  [adam_update(): master - learn_rate * (new_first / (jnp.sqrt(new_second) + epsilon) + dec...]
    unnamed x2 -> x13, local copies, waits for them, and re-layouts: 0.01 us -> 13.8 us
    convert_element_type x6 -> x1, other arithmetic: 22.6 us -> 9.28 us  [exchange(): copies[i].astype(jnp.float32)]
  transfers between devices with their start and end apart: 5 -> 0, of which waited for: 4 -> 0; matrix products, arithmetic and copies ran while one was open for 7% -> 0% of each run, Pallas kernels for 0% -> 0%
where the time goes in v2:
time: 489 us; the launch traced here: 488 us
  Pallas kernels  407 us (83%)
  matrix products  45.7 us (9%)
  local copies, waits for them, and re-layouts  13.8 us (3%)
  other arithmetic  9.29 us (2%)
  blocking collectives  9.11 us (2%)
    pallas_call x1, Pallas kernels, exchange(): pl.pallas_call(partial(kernel, chips, groups, chunks, distance), out_shap...  407 us
    dot_general x1, matrix products, body(): jnp.dot(next_input, gathered.reshape(members * rows, columns), preferred_...  23.2 us
    dot_general x1, matrix products, body(): lax.dot_general(activations, masked, (((0,), (0,)), ((), ())), preferred_...  22.5 us
    unnamed x13, local copies, waits for them, and re-layouts  13.8 us

profile of v2, /device:TPU:8, one launch (start us, length us, event | category | flops | bytes accessed | tf_op | source)
XLA Modules:
  0.0 488.1 jit_solution(15110222763324036164)
XLA Ops:
  1.3 9.1 %psum.7 = s32[]{:T(128)} all-reduce(s32[]{:T(128)} %bitcast.1), channel_id=1, replica_groups=mesh['dp'=4,'fsdp'=8] {'fsdp'}, use_global_device_ids=true, to_apply=%region_0.0 | all-reduce | flops 1 | bytes 8 | tf_op jit(solution)/shard_map/psum | solution.py:355
  11.7 22.5 %convolution_convert_fusion = bf16[3584,4096]{0,1:T(8,128)(2,1)} fusion(bf16[512,4096]{1,0:T(8,128)(2,1)} %param.12, bf16[512,3584]{1,0:T(8,128)(2,1)} %param.13, pred[512]{0:T(512)(128)(4,1)S(1)} %iota_compare_fusion), kind=kOutput, calls=%fused_computation | convolution fusion | flops 15048900608 | bytes 37224960 | tf_op jit(solution)/shard_map/dot_general | solution.py:358
  34.2 407.6 %conditional.1 = ((bf16[4,2,512,3584]{3,2,1,0:T(8,128)(2,1)}, f32[512,3584]{1,0:T(8,128)}, f32[512,3584]{1,0:T(8,128)}, f32[512,3584]{1,0:T(8,128)}, bf16[3,512,3584]{2,1,0:T(8,128)(2,1)})) conditional(s32[]{:T(128)} %bitcast, (f32[1]{0:T(128)}, bf16[4,2,512,3584]{3,2,1,0:T(8,128)(2,1)}, bf16[512,3584]{1,0:T(8,128)(2,1)}, ...), branch_computations={%region_1.2_spmd.clone, %region_2.3_spmd.clone, %region_3.4_spmd.c... | conditional | bytes 8 | solution.py:363
  34.2 407.4 %exchange_3.2 = (bf16[4,2,512,3584]{3,2,1,0:T(8,128)(2,1)}, f32[512,3584]{1,0:T(8,128)}, f32[512,3584]{1,0:T(8,128)}, f32[512,3584]{1,0:T(8,128)}, bf16[3,512,3584]{2,1,0:T(8,128)(2,1)}) custom-call(f32[1]{0:T(128)} %get-tuple-element.127.total, bf16[4,2,512,3584]{3,2,1,0:T(8,128)(2,1)} %get-tuple-element.128.sums, ...), custom_call_target="tpu_custom_call" | custom-call | tf_op jit(solution)/shard_map/cond/branch_2_fun/exchange_3/pallas_call | solution.py:305
  441.8 0.0 copy-start
  441.8 23.2 %fusion = bf16[512,3584]{1,0:T(8,128)(2,1)} fusion(bf16[512,4096]{1,0:T(8,128)(2,1)} %param.14, bf16[4096,3584]{1,0:T(8,128)(2,1)} %bitcast.28), kind=kOutput, calls=%fused_computation.2 | convolution fusion | flops 15034220544 | bytes 37224448 | tf_op jit(solution)/shard_map/dot_general | solution.py:367
  465.0 0.0 copy-done
  465.0 0.0 copy-start.1
  465.0 9.3 %bitcast_convert_fusion = (f32[512,3584]{1,0:T(8,128)}, f32[512,3584]{1,0:T(8,128)}, f32[512,3584]{1,0:T(8,128)}) fusion(bf16[3,512,3584]{2,1,0:T(8,128)(2,1)S(1)} %copy-done), kind=kLoop, calls=%fused_computation.3 | loop fusion | flops 5505024 | bytes 33030144 | tf_op jit(solution)/shard_map/cond/branch_0_fun/convert_element_type | solution.py:337
  474.3 0.0 copy-done.1
  474.3 0.0 copy-start.2
  474.3 0.0 slice-start
  474.3 3.7 copy.35
  478.0 2.0 copy-done.2
  480.0 0.0 slice-start.1
  480.0 3.7 copy.36
  483.8 0.0 slice-done
  483.8 1.3 slice-done.1
  485.0 3.0 copy.37
  (2 shorter events, 0.0 us)
Async XLA Ops:
  441.8 23.2 %copy-start = (bf16[3,512,3584]{2,1,0:T(8,128)(2,1)S(1)}, bf16[3,512,3584]{2,1,0:T(8,128)(2,1)}, u32[]{:S(2)}) copy-start(bf16[3,512,3584]{2,1,0:T(8,128)(2,1)} %get-tuple-element.94) | copy-start | bytes 33030148
  465.0 9.3 %copy-start.1 = (f32[512,3584]{1,0:T(8,128)S(1)}, f32[512,3584]{1,0:T(8,128)}, u32[]{:S(2)}) copy-start(f32[512,3584]{1,0:T(8,128)} %get-tuple-element.169) | copy-start | bytes 22020100
  474.3 5.7 %copy-start.2 = (f32[512,3584]{1,0:T(8,128)S(1)}, f32[512,3584]{1,0:T(8,128)}, u32[]{:S(2)}) copy-start(f32[512,3584]{1,0:T(8,128)} %get-tuple-element.170) | copy-start | bytes 22020100
  474.3 9.5 %slice-start = ((s8[7340032]{0:T(1024)(128)(4,1)}), s8[4194304]{0:T(1024)(128)(4,1)S(1)}, s32[]{:S(2)}) async-start(s8[7340032]{0:T(1024)(128)(4,1)} %bitcast.26), calls=%async_computation | async-start | bytes 8388608
  480.0 5.0 %slice-start.1 = ((s8[7340032]{0:T(1024)(128)(4,1)}), s8[3145728]{0:T(1024)(128)(4,1)S(1)}, s32[]{:S(2)}) async-start(s8[7340032]{0:T(1024)(128)(4,1)} %bitcast.26), calls=%async_computation.1 | async-start | bytes 6291456

commit v3 on v2

--- a/solution.py
+++ b/solution.py
@@ -15,7 +15,7 @@
 decay_rate = 0.1
 
 MESH = pl.DeviceIdType.MESH
-WIDTH = 256
+WIDTH = 128
 HOP = 2
 PARTS = 8
 

time: 489 us -> 451 us (0.922)
  Pallas kernels: 407 us -> 370 us
    pallas_call x1, Pallas kernels: 407 us -> 370 us  [exchange(): pl.pallas_call(partial(kernel, chips, groups, chunks, distance), out_shap...]
where the time goes in v3:
time: 451 us
  Pallas kernels  370 us (82%)
  matrix products  45.7 us (10%)
  local copies, waits for them, and re-layouts  13.8 us (3%)
  other arithmetic  9.29 us (2%)
  blocking collectives  9.11 us (2%)
    pallas_call x1, Pallas kernels, exchange(): pl.pallas_call(partial(kernel, chips, groups, chunks, distance), out_shap...  370 us
    dot_general x1, matrix products, body(): jnp.dot(next_input, gathered.reshape(members * rows, columns), preferred_...  23.2 us
    dot_general x1, matrix products, body(): lax.dot_general(activations, masked, (((0,), (0,)), ((), ())), preferred_...  22.5 us
    unnamed x13, local copies, waits for them, and re-layouts  13.8 us
    convert_element_type x1, other arithmetic, exchange(): copies[i].astype(jnp.float32)  9.28 us
    psum x1, blocking collectives, body(): token_total = lax.psum(own_count, 'fsdp').astype(jnp.float32).reshape(1)  9.11 us

profile of v3, /device:TPU:8, one launch (start us, length us, event | category | flops | bytes accessed | tf_op | source)
XLA Modules:
  0.0 451.1 jit_solution(14373601487938459994)
XLA Ops:
  1.3 9.1 %psum.7 = s32[]{:T(128)} all-reduce(s32[]{:T(128)} %bitcast.1), channel_id=1, replica_groups=mesh['dp'=4,'fsdp'=8] {'fsdp'}, use_global_device_ids=true, to_apply=%region_0.0 | all-reduce | flops 1 | bytes 8 | tf_op jit(solution)/shard_map/psum | solution.py:355
  11.7 22.5 %convolution_convert_fusion = bf16[3584,4096]{0,1:T(8,128)(2,1)} fusion(bf16[512,4096]{1,0:T(8,128)(2,1)} %param.12, bf16[512,3584]{1,0:T(8,128)(2,1)} %param.13, pred[512]{0:T(512)(128)(4,1)S(1)} %iota_compare_fusion), kind=kOutput, calls=%fused_computation | convolution fusion | flops 15048900608 | bytes 37224960 | tf_op jit(solution)/shard_map/dot_general | solution.py:358
  34.2 370.6 %conditional.1 = ((bf16[4,2,512,3584]{3,2,1,0:T(8,128)(2,1)}, f32[512,3584]{1,0:T(8,128)}, f32[512,3584]{1,0:T(8,128)}, f32[512,3584]{1,0:T(8,128)}, bf16[3,512,3584]{2,1,0:T(8,128)(2,1)})) conditional(s32[]{:T(128)} %bitcast, (f32[1]{0:T(128)}, bf16[4,2,512,3584]{3,2,1,0:T(8,128)(2,1)}, bf16[512,3584]{1,0:T(8,128)(2,1)}, ...), branch_computations={%region_1.2_spmd.clone, %region_2.3_spmd.clone, %region_3.4_spmd.c... | conditional | bytes 8 | solution.py:363
  34.2 370.4 %exchange_1.2 = (bf16[4,2,512,3584]{3,2,1,0:T(8,128)(2,1)}, f32[512,3584]{1,0:T(8,128)}, f32[512,3584]{1,0:T(8,128)}, f32[512,3584]{1,0:T(8,128)}, bf16[3,512,3584]{2,1,0:T(8,128)(2,1)}) custom-call(f32[1]{0:T(128)} %get-tuple-element.95.total, bf16[4,2,512,3584]{3,2,1,0:T(8,128)(2,1)} %get-tuple-element.96.sums, ...), custom_call_target="tpu_custom_call" | custom-call | tf_op jit(solution)/shard_map/cond/branch_0_fun/exchange_1/pallas_call | solution.py:305
  404.8 0.0 copy-start
  404.9 23.2 %fusion = bf16[512,3584]{1,0:T(8,128)(2,1)} fusion(bf16[512,4096]{1,0:T(8,128)(2,1)} %param.14, bf16[4096,3584]{1,0:T(8,128)(2,1)} %bitcast.28), kind=kOutput, calls=%fused_computation.2 | convolution fusion | flops 15034220544 | bytes 37224448 | tf_op jit(solution)/shard_map/dot_general | solution.py:367
  428.1 0.0 copy-done
  428.1 0.0 copy-start.1
  428.1 9.3 %bitcast_convert_fusion = (f32[512,3584]{1,0:T(8,128)}, f32[512,3584]{1,0:T(8,128)}, f32[512,3584]{1,0:T(8,128)}) fusion(bf16[3,512,3584]{2,1,0:T(8,128)(2,1)S(1)} %copy-done), kind=kLoop, calls=%fused_computation.3 | loop fusion | flops 5505024 | bytes 33030144 | tf_op jit(solution)/shard_map/cond/branch_0_fun/convert_element_type | solution.py:337
  437.4 0.0 copy-done.1
  437.4 0.0 copy-start.2
  437.4 0.0 slice-start
  437.4 3.7 copy.35
  441.1 2.0 copy-done.2
  443.1 0.0 slice-start.1
  443.1 3.7 copy.36
  446.8 0.0 slice-done
  446.8 1.3 slice-done.1
  448.1 3.0 copy.37
  (2 shorter events, 0.0 us)
Async XLA Ops:
  404.8 23.2 %copy-start = (bf16[3,512,3584]{2,1,0:T(8,128)(2,1)S(1)}, bf16[3,512,3584]{2,1,0:T(8,128)(2,1)}, u32[]{:S(2)}) copy-start(bf16[3,512,3584]{2,1,0:T(8,128)(2,1)} %get-tuple-element.94) | copy-start | bytes 33030148
  428.1 9.3 %copy-start.1 = (f32[512,3584]{1,0:T(8,128)S(1)}, f32[512,3584]{1,0:T(8,128)}, u32[]{:S(2)}) copy-start(f32[512,3584]{1,0:T(8,128)} %get-tuple-element.169) | copy-start | bytes 22020100
  437.4 5.7 %copy-start.2 = (f32[512,3584]{1,0:T(8,128)S(1)}, f32[512,3584]{1,0:T(8,128)}, u32[]{:S(2)}) copy-start(f32[512,3584]{1,0:T(8,128)} %get-tuple-element.170) | copy-start | bytes 22020100
  437.4 9.5 %slice-start = ((s8[7340032]{0:T(1024)(128)(4,1)}), s8[4194304]{0:T(1024)(128)(4,1)S(1)}, s32[]{:S(2)}) async-start(s8[7340032]{0:T(1024)(128)(4,1)} %bitcast.26), calls=%async_computation | async-start | bytes 8388608
  443.1 5.0 %slice-start.1 = ((s8[7340032]{0:T(1024)(128)(4,1)}), s8[3145728]{0:T(1024)(128)(4,1)S(1)}, s32[]{:S(2)}) async-start(s8[7340032]{0:T(1024)(128)(4,1)} %bitcast.26), calls=%async_computation.1 | async-start | bytes 6291456
